TPU v7x, 32 devices: a whole 2x2x4 slice. The times are simulated.
32 devices in a mesh: rep: 2 (over x), ctx: 8 (over z, y), tp: 2 (over core).
Axes of the slice: x: 2, y: 2, z: 4, core: 2. Of those that a mesh axis runs over, the one named last changes fastest.
Arguments:
- queries: bfloat16 [4096, 4096], P(('rep', 'ctx'), 'tp'), parts along dimension 0, may hold values from -8 to 8
- rotated_key_rows: bfloat16 [4096, 512], P(('rep', 'ctx'), 'tp'), parts along dimension 0, may hold values from -8 to 8
- ordered_value_rows: bfloat16 [4096, 512], P(('rep', 'ctx'), 'tp'), parts along dimension 0, may hold values from -6 to 6
- block_order: int32 [32], P('rep'), parts along dimension 0, may hold values from 0 to 15, each once
- live_blocks: int32 [32, 12], P('rep'), parts along dimension 0, may hold values from -1 to 15, as said below
Outputs:
- attended: bfloat16 [4096, 4096], P(('rep', 'ctx', 'tp')), parts along dimension 0
- log_norm: float32 [64, 2048], P(('rep', 'tp'), 'ctx'), parts along dimension 0
There are 2 independent parts, one for each index of `rep`. A program takes and returns all parts, laid end to end along the dimension named above; each array names one. Nothing has to cross between parts.
Inputs may be any that keep to these rules, and one draw needn't show every extreme that they name: `live_blocks`: row s names block s in its first slot, then distinct blocks before s, then -1 in every unused slot; row 15 fills all 12 slots.
All inputs are finite; a program needn't handle non-finite values.
Results may differ from a plain program's by a relative error of at most 0.008.
Values may be sent and summed in bfloat16 or wider, within the bound.
A program may use at most 128 MiB of HBM per device.

v0:
```python
import jax
import jax.numpy as jnp
from jax import lax
from jax.sharding import PartitionSpec as P

HEAD_SIZE = 128
BLOCK_TOKENS = 128
NEG_LARGE = -1e30


def body(queries, rotated_key_rows, ordered_value_rows, block_order, live_blocks):
    tok_rows = queries.shape[0]
    kv_local = rotated_key_rows.shape[1] // HEAD_SIZE
    heads_local = queries.shape[1] // HEAD_SIZE
    query_groups = heads_local // kv_local
    blocks_total = block_order.shape[0]
    blocks_here = tok_rows // BLOCK_TOKENS
    factor = HEAD_SIZE ** (-0.5)
    shard_index = lax.axis_index("ctx")
    block_ids = jnp.arange(blocks_total, dtype=jnp.int32)
    my_blocks = lax.dynamic_slice_in_dim(block_order, shard_index * blocks_here, blocks_here)
    my_lists = jnp.take(live_blocks, my_blocks, axis=0)
    live_table = jnp.any(my_lists[:, :, None] == block_ids[None, None, :], axis=1)
    within = jnp.arange(BLOCK_TOKENS, dtype=jnp.int32)
    causal_square = within[None, :] <= within[:, None]
    query_heads = queries.reshape(tok_rows, kv_local, query_groups, HEAD_SIZE)
    carried = tuple(
        (
            (
                jnp.full((kv_local, query_groups, BLOCK_TOKENS), NEG_LARGE, jnp.float32),
                jnp.zeros((kv_local, query_groups, BLOCK_TOKENS), jnp.float32),
                jnp.zeros((kv_local, query_groups, BLOCK_TOKENS, HEAD_SIZE), jnp.float32),
            )
            for block_local in range(blocks_here)
        )
    )
    key_piece = lax.all_gather(rotated_key_rows, "ctx", axis=0, tiled=True)
    value_piece = lax.all_gather(ordered_value_rows, "ctx", axis=0, tiled=True)
    key_blocks = key_piece.shape[0] // BLOCK_TOKENS

    def one_key_block(turn_index, states):
        offset = turn_index * BLOCK_TOKENS
        key_part = lax.dynamic_slice_in_dim(key_piece, offset, BLOCK_TOKENS).reshape(
            BLOCK_TOKENS, kv_local, HEAD_SIZE
        )
        value_part = lax.dynamic_slice_in_dim(value_piece, offset, BLOCK_TOKENS).reshape(
            BLOCK_TOKENS, kv_local, HEAD_SIZE
        )
        key_seq = block_order[offset // BLOCK_TOKENS]
        updated = []
        for block_local in range(blocks_here):
            query_part = query_heads[block_local * BLOCK_TOKENS : (block_local + 1) * BLOCK_TOKENS]
            allowed = (key_seq != my_blocks[block_local]) | causal_square

            def compute_tile(current):
                running, denominator, weighted = current
                scores = (
                    jnp.einsum(
                        "qhgd,khd->hgqk", query_part, key_part, preferred_element_type=jnp.float32
                    )
                    * factor
                )
                scores = jnp.where(allowed, scores, NEG_LARGE)
                new_peak = jnp.maximum(running, jnp.max(scores, axis=-1))
                weights = jnp.where(allowed, jnp.exp(scores - new_peak[..., None]), 0.0)
                rescale = jnp.exp(running - new_peak)
                denominator = denominator * rescale + jnp.sum(weights, axis=-1)
                weighted = weighted * rescale[..., None] + jnp.einsum(
                    "hgqk,khd->hgqd",
                    weights.astype(jnp.bfloat16),
                    value_part,
                    preferred_element_type=jnp.float32,
                )
                return (new_peak, denominator, weighted)

            updated.append(
                lax.cond(
                    live_table[block_local, key_seq],
                    compute_tile,
                    lambda current: current,
                    states[block_local],
                )
            )
        return tuple(updated)

    states = lax.fori_loop(0, key_blocks, one_key_block, carried)
    running = jnp.concatenate([item[0] for item in states], axis=2)
    denominator = jnp.concatenate([item[1] for item in states], axis=2)
    weighted = jnp.concatenate([item[2] for item in states], axis=2)
    normed = weighted / denominator[..., None]
    merged_out = (
        jnp.transpose(normed, (2, 0, 1, 3))
        .reshape(tok_rows, heads_local * HEAD_SIZE)
        .astype(jnp.bfloat16)
    )
    log_norm = (running + jnp.log(denominator)).reshape(heads_local, tok_rows)
    attended = lax.all_to_all(merged_out, "tp", split_axis=0, concat_axis=1, tiled=True)
    return (attended, log_norm)


def solution(mesh):
    placed = (
        P(("rep", "ctx"), "tp"),
        P(("rep", "ctx"), "tp"),
        P(("rep", "ctx"), "tp"),
        P("rep"),
        P("rep", None),
    )
    return jax.shard_map(
        body,
        mesh=mesh,
        in_specs=placed,
        out_specs=(P(("rep", "ctx", "tp"), None), P(("rep", "tp"), "ctx")),
        check_vma=False,
    )
```

profile of v0, /device:TPU:0, one launch (start us, length us, event | category | flops | bytes accessed | tf_op | source)
XLA Modules:
  0.0 250.6 jit_solution(15988656583783142846)
XLA Ops:
  7.2 1.7 copy.39
  9.0 1.7 copy.40
  10.6 1.5 copy.41
  13.7 39.1 %all-gather.3.cloned.1.call-done = bf16[2048,256]{0,1:T(8,128)(2,1)} async-done(((bf16[256,256]{0,1:T(8,128)(2,1)}), bf16[2048,256]{0,1:T(8,128)(2,1)}) %all-gather.3.cloned.1.call-update) | async-done | bytes 1048592 | tf_op jit(solution)/shard_map/all_gather | solution.py:37
  52.8 40.5 %all-gather.5.cloned.1.call-done = bf16[2048,256]{0,1:T(8,128)(2,1)} async-done(((bf16[256,256]{0,1:T(8,128)(2,1)}), bf16[2048,256]{0,1:T(8,128)(2,1)}) %all-gather.5.cloned.1.call-update) | async-done | bytes 1048592 | tf_op jit(solution)/shard_map/all_gather | solution.py:38
  93.5 141.2 %while.27 = (s32[]{:T(128)}, f32[2,8,128]{2,1,0:T(8,128)S(1)}, f32[2,8,128]{2,1,0:T(8,128)S(1)}, f32[2,8,128,128]{3,2,1,0:T(8,128)S(1)}, f32[2,8,128]{2,1,0:T(8,...) while((s32[]{:T(128)}, f32[2,8,128]{2,1,0:T(8,128)S(1)}, ...), condition=%wide.region_10.11_spmd.clone.clone, body=%wide.region_1.10_spmd.clone.clone.sunk | while | flops 274260000 | bytes 12501754 | solution.py:86
  98.0 0.9 constant_dynamic-slice_fusion.7
  98.9 2.0 conditional.8
  100.2 0.7 convolution_add_fusion
  105.4 0.9 constant_dynamic-slice_fusion.7
  106.3 3.3 %conditional.9 = ((f32[2,8,128]{2,1,0:T(8,128)S(1)}, f32[2,8,128]{2,1,0:T(8,128)S(1)}, f32[2,8,128,128]{3,2,1,0:T(8,128)S(1)})) conditional(s32[]{:T(128)} %bitcast.60, (f32[2,8,128]{2,1,0:T(8,128)S(1)}, f32[2,8,128]{2,1,0:T(8,128)S(1)}, f32[2,8,128,128]{3,2,1,0:T(8,128)S(1)}) %tuple.96, (s32[2]{0:T(128)S(1)}, s32[]{:T(128)}, ...), branch_computations={%region_6.6_spmd, %region_7.9_spmd} | conditional | flops 137121792 | bytes 6111282 | solution.py:77
  108.9 0.7 convolution_add_fusion.1
  114.2 0.9 constant_dynamic-slice_fusion.7
  115.0 2.0 conditional.8
  116.3 0.7 convolution_add_fusion
  117.1 3.3 %conditional.9 = ((f32[2,8,128]{2,1,0:T(8,128)S(1)}, f32[2,8,128]{2,1,0:T(8,128)S(1)}, f32[2,8,128,128]{3,2,1,0:T(8,128)S(1)})) conditional(s32[]{:T(128)} %bitcast.60, (f32[2,8,128]{2,1,0:T(8,128)S(1)}, f32[2,8,128]{2,1,0:T(8,128)S(1)}, f32[2,8,128,128]{3,2,1,0:T(8,128)S(1)}) %tuple.96, (s32[2]{0:T(128)S(1)}, s32[]{:T(128)}, ...), branch_computations={%region_6.6_spmd, %region_7.9_spmd} | conditional | flops 137121792 | bytes 6111282 | solution.py:77
  119.6 0.7 convolution_add_fusion.1
  124.9 0.9 constant_dynamic-slice_fusion.7
  125.8 2.0 conditional.8
  127.1 0.7 convolution_add_fusion
  127.8 3.3 %conditional.9 = ((f32[2,8,128]{2,1,0:T(8,128)S(1)}, f32[2,8,128]{2,1,0:T(8,128)S(1)}, f32[2,8,128,128]{3,2,1,0:T(8,128)S(1)})) conditional(s32[]{:T(128)} %bitcast.60, (f32[2,8,128]{2,1,0:T(8,128)S(1)}, f32[2,8,128]{2,1,0:T(8,128)S(1)}, f32[2,8,128,128]{3,2,1,0:T(8,128)S(1)}) %tuple.96, (s32[2]{0:T(128)S(1)}, s32[]{:T(128)}, ...), branch_computations={%region_6.6_spmd, %region_7.9_spmd} | conditional | flops 137121792 | bytes 6111282 | solution.py:77
  130.3 0.7 convolution_add_fusion.1
  135.6 0.9 constant_dynamic-slice_fusion.7
  136.5 2.0 conditional.8
  137.8 0.7 convolution_add_fusion
  138.5 3.3 %conditional.9 = ((f32[2,8,128]{2,1,0:T(8,128)S(1)}, f32[2,8,128]{2,1,0:T(8,128)S(1)}, f32[2,8,128,128]{3,2,1,0:T(8,128)S(1)})) conditional(s32[]{:T(128)} %bitcast.60, (f32[2,8,128]{2,1,0:T(8,128)S(1)}, f32[2,8,128]{2,1,0:T(8,128)S(1)}, f32[2,8,128,128]{3,2,1,0:T(8,128)S(1)}) %tuple.96, (s32[2]{0:T(128)S(1)}, s32[]{:T(128)}, ...), branch_computations={%region_6.6_spmd, %region_7.9_spmd} | conditional | flops 137121792 | bytes 6111282 | solution.py:77
  141.1 0.7 convolution_add_fusion.1
  146.3 0.9 constant_dynamic-slice_fusion.7
  147.2 2.0 conditional.8
  148.5 0.7 convolution_add_fusion
  149.2 3.3 %conditional.9 = ((f32[2,8,128]{2,1,0:T(8,128)S(1)}, f32[2,8,128]{2,1,0:T(8,128)S(1)}, f32[2,8,128,128]{3,2,1,0:T(8,128)S(1)})) conditional(s32[]{:T(128)} %bitcast.60, (f32[2,8,128]{2,1,0:T(8,128)S(1)}, f32[2,8,128]{2,1,0:T(8,128)S(1)}, f32[2,8,128,128]{3,2,1,0:T(8,128)S(1)}) %tuple.96, (s32[2]{0:T(128)S(1)}, s32[]{:T(128)}, ...), branch_computations={%region_6.6_spmd, %region_7.9_spmd} | conditional | flops 137121792 | bytes 6111282 | solution.py:77
  151.8 0.7 convolution_add_fusion.1
  157.0 0.9 constant_dynamic-slice_fusion.7
  162.5 0.9 constant_dynamic-slice_fusion.7
  163.4 3.3 %conditional.9 = ((f32[2,8,128]{2,1,0:T(8,128)S(1)}, f32[2,8,128]{2,1,0:T(8,128)S(1)}, f32[2,8,128,128]{3,2,1,0:T(8,128)S(1)})) conditional(s32[]{:T(128)} %bitcast.60, (f32[2,8,128]{2,1,0:T(8,128)S(1)}, f32[2,8,128]{2,1,0:T(8,128)S(1)}, f32[2,8,128,128]{3,2,1,0:T(8,128)S(1)}) %tuple.96, (s32[2]{0:T(128)S(1)}, s32[]{:T(128)}, ...), branch_computations={%region_6.6_spmd, %region_7.9_spmd} | conditional | flops 137121792 | bytes 6111282 | solution.py:77
  166.0 0.7 convolution_add_fusion.1
  171.2 0.9 constant_dynamic-slice_fusion.7
  172.1 3.3 %conditional.9 = ((f32[2,8,128]{2,1,0:T(8,128)S(1)}, f32[2,8,128]{2,1,0:T(8,128)S(1)}, f32[2,8,128,128]{3,2,1,0:T(8,128)S(1)})) conditional(s32[]{:T(128)} %bitcast.60, (f32[2,8,128]{2,1,0:T(8,128)S(1)}, f32[2,8,128]{2,1,0:T(8,128)S(1)}, f32[2,8,128,128]{3,2,1,0:T(8,128)S(1)}) %tuple.96, (s32[2]{0:T(128)S(1)}, s32[]{:T(128)}, ...), branch_computations={%region_6.6_spmd, %region_7.9_spmd} | conditional | flops 137121792 | bytes 6111282 | solution.py:77
  174.7 0.7 convolution_add_fusion.1
  179.9 0.9 constant_dynamic-slice_fusion.7
  180.8 2.0 conditional.8
  182.1 0.7 convolution_add_fusion
  182.8 3.3 %conditional.9 = ((f32[2,8,128]{2,1,0:T(8,128)S(1)}, f32[2,8,128]{2,1,0:T(8,128)S(1)}, f32[2,8,128,128]{3,2,1,0:T(8,128)S(1)})) conditional(s32[]{:T(128)} %bitcast.60, (f32[2,8,128]{2,1,0:T(8,128)S(1)}, f32[2,8,128]{2,1,0:T(8,128)S(1)}, f32[2,8,128,128]{3,2,1,0:T(8,128)S(1)}) %tuple.96, (s32[2]{0:T(128)S(1)}, s32[]{:T(128)}, ...), branch_computations={%region_6.6_spmd, %region_7.9_spmd} | conditional | flops 137121792 | bytes 6111282 | solution.py:77
  185.4 0.7 convolution_add_fusion.1
  190.6 0.9 constant_dynamic-slice_fusion.7
  191.5 2.0 conditional.8
  192.8 0.7 convolution_add_fusion
  193.5 3.3 %conditional.9 = ((f32[2,8,128]{2,1,0:T(8,128)S(1)}, f32[2,8,128]{2,1,0:T(8,128)S(1)}, f32[2,8,128,128]{3,2,1,0:T(8,128)S(1)})) conditional(s32[]{:T(128)} %bitcast.60, (f32[2,8,128]{2,1,0:T(8,128)S(1)}, f32[2,8,128]{2,1,0:T(8,128)S(1)}, f32[2,8,128,128]{3,2,1,0:T(8,128)S(1)}) %tuple.96, (s32[2]{0:T(128)S(1)}, s32[]{:T(128)}, ...), branch_computations={%region_6.6_spmd, %region_7.9_spmd} | conditional | flops 137121792 | bytes 6111282 | solution.py:77
  196.1 0.7 convolution_add_fusion.1
  201.4 0.9 constant_dynamic-slice_fusion.7
  206.8 0.9 constant_dynamic-slice_fusion.7
  207.7 3.3 %conditional.9 = ((f32[2,8,128]{2,1,0:T(8,128)S(1)}, f32[2,8,128]{2,1,0:T(8,128)S(1)}, f32[2,8,128,128]{3,2,1,0:T(8,128)S(1)})) conditional(s32[]{:T(128)} %bitcast.60, (f32[2,8,128]{2,1,0:T(8,128)S(1)}, f32[2,8,128]{2,1,0:T(8,128)S(1)}, f32[2,8,128,128]{3,2,1,0:T(8,128)S(1)}) %tuple.96, (s32[2]{0:T(128)S(1)}, s32[]{:T(128)}, ...), branch_computations={%region_6.6_spmd, %region_7.9_spmd} | conditional | flops 137121792 | bytes 6111282 | solution.py:77
  215.6 0.9 constant_dynamic-slice_fusion.7
  221.0 0.9 constant_dynamic-slice_fusion.7
  221.9 2.0 conditional.8
  223.2 0.7 convolution_add_fusion
  228.5 0.9 constant_dynamic-slice_fusion.7
  229.4 2.0 conditional.8
  230.7 0.7 convolution_add_fusion
  231.4 3.3 %conditional.9 = ((f32[2,8,128]{2,1,0:T(8,128)S(1)}, f32[2,8,128]{2,1,0:T(8,128)S(1)}, f32[2,8,128,128]{3,2,1,0:T(8,128)S(1)})) conditional(s32[]{:T(128)} %bitcast.60, (f32[2,8,128]{2,1,0:T(8,128)S(1)}, f32[2,8,128]{2,1,0:T(8,128)S(1)}, f32[2,8,128,128]{3,2,1,0:T(8,128)S(1)}) %tuple.96, (s32[2]{0:T(128)S(1)}, s32[]{:T(128)}, ...), branch_computations={%region_6.6_spmd, %region_7.9_spmd} | conditional | flops 137121792 | bytes 6111282 | solution.py:77
  233.9 0.7 convolution_add_fusion.1
  234.7 0.7 fusion.27
  236.6 4.6 %all_to_all.16 = bf16[2,128,2048]{2,1,0:T(8,128)(2,1)S(1)} all-to-all(bf16[2,128,2048]{2,1,0:T(8,128)(2,1)S(1)} %convert_element_type.44), channel_id=1, replica_groups=mesh['rep'=2,'ctx'=8,'tp'=2] {'tp'}, dimensions={0} | all-to-all | bytes 2097152 | tf_op jit(solution)/shard_map/all_to_all | solution.py:97
  241.8 1.3 copy.45
  (218 shorter events, 44.4 us)
Async XLA Ops:
  7.2 5.8 %copy-start = (s32[16,12]{1,0:T(8,128)S(1)}, s32[16,12]{1,0:T(8,128)}, u32[]{:S(2)}) copy-start(s32[16,12]{1,0:T(8,128)} %param.15) | copy-start | bytes 2308
  7.2 45.6 %all-gather.3.cloned.1.call-start = ((), (), s32[]{:S(2)}) async-start(), calls=%async_computation.1 | async-start | bytes 1179648 | tf_op jit(solution)/shard_map/all_gather | solution.py:37
  8.9 84.3 %all-gather.5.cloned.1.call-start = ((), (), s32[]{:S(2)}) async-start(), calls=%async_computation.2 | async-start | bytes 1179648 | tf_op jit(solution)/shard_map/all_gather | solution.py:38
  12.1 0.7 copy-start.1
Sparse Core Ops, SparseCore 0:
  10.6 42.1 all-gather.2
  54.8 38.3 all-gather.4
where the time goes:
time: 253 us; the launch traced here: 251 us
  waiting for transfers between devices  79.6 us (31%)
  loops' own time  74.1 us (29%)
  local copies, waits for them, and re-layouts  50.8 us (20%)
  matrix products  21 us (8%)
  between operations  14.2 us (6%)
  other arithmetic  6.35 us (3%)
  blocking collectives  4.58 us (2%)
    another operation x1, loops' own time, body(): states = lax.fori_loop(0, key_blocks, one_key_block, carried)  52.4 us
    all_gather x1, waiting for transfers between devices, body(): value_piece = lax.all_gather(ordered_value_rows, 'ctx', axis=0, tiled=True)  40.5 us
    all_gather x1, waiting for transfers between devices, body(): key_piece = lax.all_gather(rotated_key_rows, 'ctx', axis=0, tiled=True)  39.1 us
    another operation x32, loops' own time, one_key_block(): lax.cond(live_table[block_local, key_seq], compute_tile, lambda current:...  21.7 us
    dynamic_slice x16, local copies, waits for them, and re-layouts, one_key_block(): lax.dynamic_slice_in_dim(value_piece, offset, BLOCK_TOKENS)  14.3 us
    dot_general x20, matrix products, compute_tile(): jnp.einsum('hgqk,khd->hgqd', weights.astype(jnp.bfloat16), value_part, pr...  13.7 us
    dynamic_slice x16, local copies, waits for them, and re-layouts, one_key_block(): live_table[block_local, key_seq]  10.6 us
    dynamic_slice x16, local copies, waits for them, and re-layouts, one_key_block(): key_seq = block_order[offset // BLOCK_TOKENS]  9.39 us
  transfers between devices with their start and end apart: 2, of which 2 were waited for; matrix products, arithmetic and copies ran while one was open for 2% of the time, Pallas kernels for 0%

commit v1 on v0

--- a/solution.py
+++ b/solution.py
@@ -6,6 +6,17 @@
 HEAD_SIZE = 128
 BLOCK_TOKENS = 128
 NEG_LARGE = -1e30
+
+
+def around_the_ring(x, axis, along):
+    size = lax.axis_size(axis)
+    route = [(i, (i + 1) % size) for i in range(size)]
+    parts = [x]
+    for far in range(1, size):
+        parts = [lax.ppermute(parts[0], axis, route), *parts]
+    out = jnp.concatenate(parts, axis=along)
+    places = (lax.axis_index(axis) + 1) * parts[-1].shape[along]
+    return jnp.roll(out, places, axis=along)
 
 
 def body(queries, rotated_key_rows, ordered_value_rows, block_order, live_blocks):
@@ -34,7 +45,7 @@
             for block_local in range(blocks_here)
         )
     )
-    key_piece = lax.all_gather(rotated_key_rows, "ctx", axis=0, tiled=True)
+    key_piece = around_the_ring(rotated_key_rows, "ctx", 0)
     value_piece = lax.all_gather(ordered_value_rows, "ctx", axis=0, tiled=True)
     key_blocks = key_piece.shape[0] // BLOCK_TOKENS
 

time: 253 us -> 240 us (0.949)
  waiting for transfers between devices: 79.6 us -> 67.2 us
  loops' own time: 74.1 us -> 69.4 us
  starting transfers between devices: 0.08 us -> 3.1 us
    ppermute x0 -> x7, waiting for transfers between devices: none -> 49.1 us  [around_the_ring(): parts = [lax.ppermute(parts[0], axis, route), *parts]]
    all_gather x1 -> x0, waiting for transfers between devices: 39.1 us -> none  [body(): key_piece = lax.all_gather(rotated_key_rows, 'ctx', axis=0, tiled=True)]
    all_gather x1, waiting for transfers between devices: 40.5 us -> 18.1 us  [body(): value_piece = lax.all_gather(ordered_value_rows, 'ctx', axis=0, tiled=True)]
    another operation x1, loops' own time: 52.4 us -> 48.8 us  [body(): states = lax.fori_loop(0, key_blocks, one_key_block, carried)]
    ppermute x0 -> x7, starting transfers between devices: none -> 3.06 us  [around_the_ring(): parts = [lax.ppermute(parts[0], axis, route), *parts]]
    unnamed x9 -> x24, local copies, waits for them, and re-layouts: 6.79 us -> 6.28 us
  transfers between devices with their start and end apart: 2 -> 8, of which waited for: 2 -> 8; matrix products, arithmetic and copies ran while one was open for 2% -> 3% of each run, Pallas kernels for 0% -> 0%
where the time goes in v1:
time: 240 us; the launch traced here: 238 us
  loops' own time  69.4 us (29%)
  waiting for transfers between devices  67.2 us (28%)
  local copies, waits for them, and re-layouts  51.3 us (21%)
  matrix products  21 us (9%)
  between operations  14.3 us (6%)
  other arithmetic  6.99 us (3%)
  blocking collectives  4.58 us (2%)
  starting transfers between devices  3.1 us (1%)
    ppermute x7, waiting for transfers between devices, around_the_ring(): parts = [lax.ppermute(parts[0], axis, route), *parts]  49.1 us
    another operation x1, loops' own time, body(): states = lax.fori_loop(0, key_blocks, one_key_block, carried)  48.8 us
    another operation x32, loops' own time, one_key_block(): lax.cond(live_table[block_local, key_seq], compute_tile, lambda current:...  20.6 us
    all_gather x1, waiting for transfers between devices, body(): value_piece = lax.all_gather(ordered_value_rows, 'ctx', axis=0, tiled=True)  18.1 us
    dynamic_slice x16, local copies, waits for them, and re-layouts, one_key_block(): lax.dynamic_slice_in_dim(value_piece, offset, BLOCK_TOKENS)  14.2 us
    dot_general x20, matrix products, compute_tile(): jnp.einsum('hgqk,khd->hgqd', weights.astype(jnp.bfloat16), value_part, pr...  13.7 us
    dynamic_slice x16, local copies, waits for them, and re-layouts, one_key_block(): live_table[block_local, key_seq]  10.6 us
    dynamic_slice x16, local copies, waits for them, and re-layouts, one_key_block(): key_seq = block_order[offset // BLOCK_TOKENS]  9.25 us
  transfers between devices with their start and end apart: 8, of which 8 were waited for; matrix products, arithmetic and copies ran while one was open for 3% of the time, Pallas kernels for 0%

profile of v1, /device:TPU:0, one launch (start us, length us, event | category | flops | bytes accessed | tf_op | source)
XLA Modules:
  0.0 237.9 jit_solution(8729510954161521761)
XLA Ops:
  7.2 1.0 copy.43
  8.2 3.0 %collective-permute-start = (bf16[256,256]{0,1:T(8,128)(2,1)S(1)}, bf16[256,256]{0,1:T(8,128)(2,1)S(1)}, u32[]{:S(2)}, u32[]{:S(2)}) collective-permute-start(bf16[256,256]{0,1:T(8,128)(2,1)S(1)} %copy.43), channel_id=1, source_target_pairs={{0,2},{2,4},{4,6},{6,8},{8,10},{10,12},{12,14},{14,0},{1,3},{3,5},... | collective-permute-start | bytes 393224 | tf_op jit(solution)/shard_map/ppermute | solution.py:16
  11.3 6.5 %collective-permute-done = bf16[256,256]{0,1:T(8,128)(2,1)S(1)} collective-permute-done((bf16[256,256]{0,1:T(8,128)(2,1)S(1)}, bf16[256,256]{0,1:T(8,128)(2,1)S(1)}, u32[]{:S(2)}, u32[]{:S(2)}) %collective-permute-start) | collective-permute-done | bytes 131104 | tf_op jit(solution)/shard_map/ppermute | solution.py:16
  17.8 7.7 %collective-permute-done.1 = bf16[256,256]{0,1:T(8,128)(2,1)S(1)} collective-permute-done((bf16[256,256]{0,1:T(8,128)(2,1)S(1)}, bf16[256,256]{0,1:T(8,128)(2,1)S(1)}, u32[]{:S(2)}, u32[]{:S(2)}) %collective-permute-start.1) | collective-permute-done | bytes 131104 | tf_op jit(solution)/shard_map/ppermute | solution.py:16
  25.5 7.7 %collective-permute-done.2 = bf16[256,256]{0,1:T(8,128)(2,1)S(1)} collective-permute-done((bf16[256,256]{0,1:T(8,128)(2,1)S(1)}, bf16[256,256]{0,1:T(8,128)(2,1)S(1)}, u32[]{:S(2)}, u32[]{:S(2)}) %collective-permute-start.2) | collective-permute-done | bytes 131104 | tf_op jit(solution)/shard_map/ppermute | solution.py:16
  33.2 7.7 %collective-permute-done.3 = bf16[256,256]{0,1:T(8,128)(2,1)S(1)} collective-permute-done((bf16[256,256]{0,1:T(8,128)(2,1)S(1)}, bf16[256,256]{0,1:T(8,128)(2,1)S(1)}, u32[]{:S(2)}, u32[]{:S(2)}) %collective-permute-start.3) | collective-permute-done | bytes 131104 | tf_op jit(solution)/shard_map/ppermute | solution.py:16
  40.8 1.6 copy.46
  42.5 0.7 compare_and_fusion
  43.2 5.3 %collective-permute-done.4 = bf16[256,256]{0,1:T(8,128)(2,1)S(1)} collective-permute-done((bf16[256,256]{0,1:T(8,128)(2,1)S(1)}, bf16[256,256]{0,1:T(8,128)(2,1)S(1)}, u32[]{:S(2)}, u32[]{:S(2)}) %collective-permute-start.4) | collective-permute-done | bytes 131104 | tf_op jit(solution)/shard_map/ppermute | solution.py:16
  49.1 8.5 %collective-permute-done.5 = bf16[256,256]{0,1:T(8,128)(2,1)S(1)} collective-permute-done((bf16[256,256]{0,1:T(8,128)(2,1)S(1)}, bf16[256,256]{0,1:T(8,128)(2,1)S(1)}, u32[]{:S(2)}, u32[]{:S(2)}) %collective-permute-start.5) | collective-permute-done | bytes 131104 | tf_op jit(solution)/shard_map/ppermute | solution.py:16
  57.6 1.5 copy.47
  59.9 5.8 %collective-permute-done.6 = bf16[256,256]{0,1:T(8,128)(2,1)S(1)} collective-permute-done((bf16[256,256]{0,1:T(8,128)(2,1)S(1)}, bf16[256,256]{0,1:T(8,128)(2,1)S(1)}, u32[]{:S(2)}, u32[]{:S(2)}) %collective-permute-start.6) | collective-permute-done | bytes 131104 | tf_op jit(solution)/shard_map/ppermute | solution.py:16
  66.0 1.0 constant_dynamic-slice_fusion.4
  67.1 18.1 %all-gather.2.cloned.1.call-done = bf16[2048,256]{0,1:T(8,128)(2,1)} async-done(((bf16[256,256]{0,1:T(8,128)(2,1)}), bf16[2048,256]{0,1:T(8,128)(2,1)}) %all-gather.2.cloned.1.call-update) | async-done | bytes 1048592 | tf_op jit(solution)/shard_map/all_gather | solution.py:49
  85.4 136.5 %while.27 = (s32[]{:T(128)}, f32[2,8,128]{2,1,0:T(8,128)S(1)}, f32[2,8,128]{2,1,0:T(8,128)S(1)}, f32[2,8,128,128]{3,2,1,0:T(8,128)S(1)}, f32[2,8,128]{2,1,0:T(8,...) while((s32[]{:T(128)}, f32[2,8,128]{2,1,0:T(8,128)S(1)}, ...), condition=%wide.region_10.11_spmd.clone.clone, body=%wide.region_1.10_spmd.clone.clone.sunk | while | flops 274260000 | bytes 12501762 | solution.py:97
  89.0 0.9 constant_dynamic-slice_fusion.8
  89.9 1.9 conditional.8
  91.1 0.7 convolution_add_fusion
  96.1 0.9 constant_dynamic-slice_fusion.8
  97.7 3.3 %conditional.9 = ((f32[2,8,128]{2,1,0:T(8,128)S(1)}, f32[2,8,128]{2,1,0:T(8,128)S(1)}, f32[2,8,128,128]{3,2,1,0:T(8,128)S(1)})) conditional(s32[]{:T(128)} %bitcast.60, (f32[2,8,128]{2,1,0:T(8,128)S(1)}, f32[2,8,128]{2,1,0:T(8,128)S(1)}, f32[2,8,128,128]{3,2,1,0:T(8,128)S(1)}) %tuple.96, (s32[2]{0:T(128)S(1)}, s32[]{:T(128)}, ...), branch_computations={%region_6.6_spmd, %region_7.9_spmd} | conditional | flops 137121792 | bytes 6111282 | solution.py:88
  100.3 0.7 convolution_add_fusion.1
  104.6 0.9 constant_dynamic-slice_fusion.8
  105.5 1.9 conditional.8
  106.7 0.7 convolution_add_fusion
  108.1 3.3 %conditional.9 = ((f32[2,8,128]{2,1,0:T(8,128)S(1)}, f32[2,8,128]{2,1,0:T(8,128)S(1)}, f32[2,8,128,128]{3,2,1,0:T(8,128)S(1)})) conditional(s32[]{:T(128)} %bitcast.60, (f32[2,8,128]{2,1,0:T(8,128)S(1)}, f32[2,8,128]{2,1,0:T(8,128)S(1)}, f32[2,8,128,128]{3,2,1,0:T(8,128)S(1)}) %tuple.96, (s32[2]{0:T(128)S(1)}, s32[]{:T(128)}, ...), branch_computations={%region_6.6_spmd, %region_7.9_spmd} | conditional | flops 137121792 | bytes 6111282 | solution.py:88
  115.0 0.9 constant_dynamic-slice_fusion.8
  115.9 1.9 conditional.8
  117.1 0.7 convolution_add_fusion
  118.5 3.3 %conditional.9 = ((f32[2,8,128]{2,1,0:T(8,128)S(1)}, f32[2,8,128]{2,1,0:T(8,128)S(1)}, f32[2,8,128,128]{3,2,1,0:T(8,128)S(1)})) conditional(s32[]{:T(128)} %bitcast.60, (f32[2,8,128]{2,1,0:T(8,128)S(1)}, f32[2,8,128]{2,1,0:T(8,128)S(1)}, f32[2,8,128,128]{3,2,1,0:T(8,128)S(1)}) %tuple.96, (s32[2]{0:T(128)S(1)}, s32[]{:T(128)}, ...), branch_computations={%region_6.6_spmd, %region_7.9_spmd} | conditional | flops 137121792 | bytes 6111282 | solution.py:88
  125.4 0.9 constant_dynamic-slice_fusion.8
  126.2 1.9 conditional.8
  127.5 0.7 convolution_add_fusion
  128.8 3.3 %conditional.9 = ((f32[2,8,128]{2,1,0:T(8,128)S(1)}, f32[2,8,128]{2,1,0:T(8,128)S(1)}, f32[2,8,128,128]{3,2,1,0:T(8,128)S(1)})) conditional(s32[]{:T(128)} %bitcast.60, (f32[2,8,128]{2,1,0:T(8,128)S(1)}, f32[2,8,128]{2,1,0:T(8,128)S(1)}, f32[2,8,128,128]{3,2,1,0:T(8,128)S(1)}) %tuple.96, (s32[2]{0:T(128)S(1)}, s32[]{:T(128)}, ...), branch_computations={%region_6.6_spmd, %region_7.9_spmd} | conditional | flops 137121792 | bytes 6111282 | solution.py:88
  131.4 0.7 convolution_add_fusion.1
  135.7 0.9 constant_dynamic-slice_fusion.8
  136.6 1.9 conditional.8
  139.2 3.3 %conditional.9 = ((f32[2,8,128]{2,1,0:T(8,128)S(1)}, f32[2,8,128]{2,1,0:T(8,128)S(1)}, f32[2,8,128,128]{3,2,1,0:T(8,128)S(1)})) conditional(s32[]{:T(128)} %bitcast.60, (f32[2,8,128]{2,1,0:T(8,128)S(1)}, f32[2,8,128]{2,1,0:T(8,128)S(1)}, f32[2,8,128,128]{3,2,1,0:T(8,128)S(1)}) %tuple.96, (s32[2]{0:T(128)S(1)}, s32[]{:T(128)}, ...), branch_computations={%region_6.6_spmd, %region_7.9_spmd} | conditional | flops 137121792 | bytes 6111282 | solution.py:88
  146.1 0.9 constant_dynamic-slice_fusion.8
  151.3 0.9 constant_dynamic-slice_fusion.8
  152.9 3.3 %conditional.9 = ((f32[2,8,128]{2,1,0:T(8,128)S(1)}, f32[2,8,128]{2,1,0:T(8,128)S(1)}, f32[2,8,128,128]{3,2,1,0:T(8,128)S(1)})) conditional(s32[]{:T(128)} %bitcast.60, (f32[2,8,128]{2,1,0:T(8,128)S(1)}, f32[2,8,128]{2,1,0:T(8,128)S(1)}, f32[2,8,128,128]{3,2,1,0:T(8,128)S(1)}) %tuple.96, (s32[2]{0:T(128)S(1)}, s32[]{:T(128)}, ...), branch_computations={%region_6.6_spmd, %region_7.9_spmd} | conditional | flops 137121792 | bytes 6111282 | solution.py:88
  159.8 0.9 constant_dynamic-slice_fusion.8
  161.4 3.3 %conditional.9 = ((f32[2,8,128]{2,1,0:T(8,128)S(1)}, f32[2,8,128]{2,1,0:T(8,128)S(1)}, f32[2,8,128,128]{3,2,1,0:T(8,128)S(1)})) conditional(s32[]{:T(128)} %bitcast.60, (f32[2,8,128]{2,1,0:T(8,128)S(1)}, f32[2,8,128]{2,1,0:T(8,128)S(1)}, f32[2,8,128,128]{3,2,1,0:T(8,128)S(1)}) %tuple.96, (s32[2]{0:T(128)S(1)}, s32[]{:T(128)}, ...), branch_computations={%region_6.6_spmd, %region_7.9_spmd} | conditional | flops 137121792 | bytes 6111282 | solution.py:88
  164.0 0.7 convolution_add_fusion.1
  168.3 0.9 constant_dynamic-slice_fusion.8
  169.2 1.9 conditional.8
  170.4 0.7 convolution_add_fusion
  171.8 3.3 %conditional.9 = ((f32[2,8,128]{2,1,0:T(8,128)S(1)}, f32[2,8,128]{2,1,0:T(8,128)S(1)}, f32[2,8,128,128]{3,2,1,0:T(8,128)S(1)})) conditional(s32[]{:T(128)} %bitcast.60, (f32[2,8,128]{2,1,0:T(8,128)S(1)}, f32[2,8,128]{2,1,0:T(8,128)S(1)}, f32[2,8,128,128]{3,2,1,0:T(8,128)S(1)}) %tuple.96, (s32[2]{0:T(128)S(1)}, s32[]{:T(128)}, ...), branch_computations={%region_6.6_spmd, %region_7.9_spmd} | conditional | flops 137121792 | bytes 6111282 | solution.py:88
  174.4 0.7 convolution_add_fusion.1
  178.7 0.9 constant_dynamic-slice_fusion.8
  179.6 1.9 conditional.8
  182.2 3.3 %conditional.9 = ((f32[2,8,128]{2,1,0:T(8,128)S(1)}, f32[2,8,128]{2,1,0:T(8,128)S(1)}, f32[2,8,128,128]{3,2,1,0:T(8,128)S(1)})) conditional(s32[]{:T(128)} %bitcast.60, (f32[2,8,128]{2,1,0:T(8,128)S(1)}, f32[2,8,128]{2,1,0:T(8,128)S(1)}, f32[2,8,128,128]{3,2,1,0:T(8,128)S(1)}) %tuple.96, (s32[2]{0:T(128)S(1)}, s32[]{:T(128)}, ...), branch_computations={%region_6.6_spmd, %region_7.9_spmd} | conditional | flops 137121792 | bytes 6111282 | solution.py:88
  184.7 0.7 convolution_add_fusion.1
  189.0 0.9 constant_dynamic-slice_fusion.8
  194.3 0.9 constant_dynamic-slice_fusion.8
  195.9 3.3 %conditional.9 = ((f32[2,8,128]{2,1,0:T(8,128)S(1)}, f32[2,8,128]{2,1,0:T(8,128)S(1)}, f32[2,8,128,128]{3,2,1,0:T(8,128)S(1)})) conditional(s32[]{:T(128)} %bitcast.60, (f32[2,8,128]{2,1,0:T(8,128)S(1)}, f32[2,8,128]{2,1,0:T(8,128)S(1)}, f32[2,8,128,128]{3,2,1,0:T(8,128)S(1)}) %tuple.96, (s32[2]{0:T(128)S(1)}, s32[]{:T(128)}, ...), branch_computations={%region_6.6_spmd, %region_7.9_spmd} | conditional | flops 137121792 | bytes 6111282 | solution.py:88
  202.8 0.9 constant_dynamic-slice_fusion.8
  208.0 0.9 constant_dynamic-slice_fusion.8
  208.9 1.9 conditional.8
  215.1 0.9 constant_dynamic-slice_fusion.8
  216.0 1.9 conditional.8
  218.6 3.3 %conditional.9 = ((f32[2,8,128]{2,1,0:T(8,128)S(1)}, f32[2,8,128]{2,1,0:T(8,128)S(1)}, f32[2,8,128,128]{3,2,1,0:T(8,128)S(1)})) conditional(s32[]{:T(128)} %bitcast.60, (f32[2,8,128]{2,1,0:T(8,128)S(1)}, f32[2,8,128]{2,1,0:T(8,128)S(1)}, f32[2,8,128,128]{3,2,1,0:T(8,128)S(1)}) %tuple.96, (s32[2]{0:T(128)S(1)}, s32[]{:T(128)}, ...), branch_computations={%region_6.6_spmd, %region_7.9_spmd} | conditional | flops 137121792 | bytes 6111282 | solution.py:88
  221.9 0.7 fusion.27
  223.8 4.6 %all_to_all.16 = bf16[2,128,2048]{2,1,0:T(8,128)(2,1)S(1)} all-to-all(bf16[2,128,2048]{2,1,0:T(8,128)(2,1)S(1)} %convert_element_type.44), channel_id=1, replica_groups=mesh['rep'=2,'ctx'=8,'tp'=2] {'tp'}, dimensions={0} | all-to-all | bytes 2097152 | tf_op jit(solution)/shard_map/all_to_all | solution.py:108
  229.1 1.3 copy.51
  (246 shorter events, 50.6 us)
Async XLA Ops:
  7.2 41.4 %copy-start = (s32[16,12]{1,0:T(8,128)S(1)}, s32[16,12]{1,0:T(8,128)}, u32[]{:S(2)}) copy-start(s32[16,12]{1,0:T(8,128)} %param.15) | copy-start | bytes 2308
  7.2 78.0 %all-gather.2.cloned.1.call-start = ((), (), s32[]{:S(2)}) async-start(), calls=%async_computation.1 | async-start | bytes 1179648 | tf_op jit(solution)/shard_map/all_gather | solution.py:49
  8.2 9.6 %collective-permute-start = (bf16[256,256]{0,1:T(8,128)(2,1)S(1)}, bf16[256,256]{0,1:T(8,128)(2,1)S(1)}, u32[]{:S(2)}, u32[]{:S(2)}) collective-permute-start(bf16[256,256]{0,1:T(8,128)(2,1)S(1)} %copy.43), channel_id=1, source_target_pairs={{0,2},{2,4},{4,6},{6,8},{8,10},{10,12},{12,14},{14,0},{1,3},{3,5},... | collective-permute-start | bytes 393224 | tf_op jit(solution)/shard_map/ppermute | solution.py:16
  17.8 7.7 %collective-permute-start.1 = (bf16[256,256]{0,1:T(8,128)(2,1)S(1)}, bf16[256,256]{0,1:T(8,128)(2,1)S(1)}, u32[]{:S(2)}, u32[]{:S(2)}) collective-permute-start(bf16[256,256]{0,1:T(8,128)(2,1)S(1)} %collective-permute-done), channel_id=1, source_target_pairs={{0,2},{2,4},{4,6},{6,8},{8,10},{10,12},{12,14},{14,0},{1,3},{3,5},... | collective-permute-start | bytes 393224 | tf_op jit(solution)/shard_map/ppermute | solution.py:16
  25.5 7.7 %collective-permute-start.2 = (bf16[256,256]{0,1:T(8,128)(2,1)S(1)}, bf16[256,256]{0,1:T(8,128)(2,1)S(1)}, u32[]{:S(2)}, u32[]{:S(2)}) collective-permute-start(bf16[256,256]{0,1:T(8,128)(2,1)S(1)} %collective-permute-done.1), channel_id=1, source_target_pairs={{0,2},{2,4},{4,6},{6,8},{8,10},{10,12},{12,14},{14,0},{1,3},{3,5},... | collective-permute-start | bytes 393224 | tf_op jit(solution)/shard_map/ppermute | solution.py:16
  33.1 7.7 %collective-permute-start.3 = (bf16[256,256]{0,1:T(8,128)(2,1)S(1)}, bf16[256,256]{0,1:T(8,128)(2,1)S(1)}, u32[]{:S(2)}, u32[]{:S(2)}) collective-permute-start(bf16[256,256]{0,1:T(8,128)(2,1)S(1)} %collective-permute-done.2), channel_id=1, source_target_pairs={{0,2},{2,4},{4,6},{6,8},{8,10},{10,12},{12,14},{14,0},{1,3},{3,5},... | collective-permute-start | bytes 393224 | tf_op jit(solution)/shard_map/ppermute | solution.py:16
  40.8 7.7 %collective-permute-start.4 = (bf16[256,256]{0,1:T(8,128)(2,1)S(1)}, bf16[256,256]{0,1:T(8,128)(2,1)S(1)}, u32[]{:S(2)}, u32[]{:S(2)}) collective-permute-start(bf16[256,256]{0,1:T(8,128)(2,1)S(1)} %collective-permute-done.3), channel_id=1, source_target_pairs={{0,2},{2,4},{4,6},{6,8},{8,10},{10,12},{12,14},{14,0},{1,3},{3,5},... | collective-permute-start | bytes 393224 | tf_op jit(solution)/shard_map/ppermute | solution.py:16
  48.5 9.0 %collective-permute-start.5 = (bf16[256,256]{0,1:T(8,128)(2,1)S(1)}, bf16[256,256]{0,1:T(8,128)(2,1)S(1)}, u32[]{:S(2)}, u32[]{:S(2)}) collective-permute-start(bf16[256,256]{0,1:T(8,128)(2,1)S(1)} %collective-permute-done.4), channel_id=1, source_target_pairs={{0,2},{2,4},{4,6},{6,8},{8,10},{10,12},{12,14},{14,0},{1,3},{3,5},... | collective-permute-start | bytes 393224 | tf_op jit(solution)/shard_map/ppermute | solution.py:16
  57.6 8.2 %collective-permute-start.6 = (bf16[256,256]{0,1:T(8,128)(2,1)S(1)}, bf16[256,256]{0,1:T(8,128)(2,1)S(1)}, u32[]{:S(2)}, u32[]{:S(2)}) collective-permute-start(bf16[256,256]{0,1:T(8,128)(2,1)S(1)} %collective-permute-done.5), channel_id=1, source_target_pairs={{0,2},{2,4},{4,6},{6,8},{8,10},{10,12},{12,14},{14,0},{1,3},{3,5},... | collective-permute-start | bytes 393224 | tf_op jit(solution)/shard_map/ppermute | solution.py:16
  66.0 19.3 %copy-start.1 = (s32[16]{0:T(128)S(1)}, s32[16]{0:T(128)}, u32[]{:S(2)}) copy-start(s32[16]{0:T(128)} %param.14) | copy-start | bytes 196
Sparse Core Ops, SparseCore 0:
  42.6 42.4 all-gather.1
